TPU v7x, 256 devices: a whole 4x4x8 slice. The times are simulated.
256 devices in a mesh: tm: 64 (over z_hi, y, x), head: 4 (over z_lo, core).
Axes of the slice: x: 4, y: 4, z: 8 (z_hi: 4, z_lo: 2; z = z_hi * 2 + z_lo), core: 2. Of those that a mesh axis runs over, the one named last changes fastest.
Arguments:
- query: bfloat16 [16384, 4096], P('tm', 'head'), may hold values from -200 to 200
- key_in: bfloat16 [16384, 4096], P('tm', 'head'), may hold values from -7 to 7
- value: bfloat16 [16384, 4096], P('tm', 'head'), may hold values from -6 to 6
- grad_out: bfloat16 [16384, 4096], P('tm', 'head'), may hold values from -6 to 6
- weights: bfloat16 [3, 4096, 4096], P(None, 'tm', 'head'), may hold values from -0.09375 to 0.09375
Outputs:
- grad_input_t: bfloat16 [4096, 16384], P('head', 'tm')
All inputs are finite; a program needn't handle non-finite values.
Results may differ from a plain program's by a relative error of at most 0.0091.
Values may be sent and summed in bfloat16 or wider, within the bound.
A program may use at most 256 MiB of HBM per device.

v0:
```python
import jax
import jax.numpy as jnp
from jax import lax
from jax.sharding import PartitionSpec as P

HD = 128


def temporal(q_heads, k_heads, v_heads, g_heads):
    scale = 1.0 / q_heads.shape[-1] ** 0.5
    scores = (
        jnp.einsum("fphd,gphd->phfg", q_heads, k_heads, preferred_element_type=jnp.float32) * scale
    )
    probs = jax.nn.softmax(scores, axis=-1)
    probs_b = probs.astype(jnp.bfloat16)
    attended = jnp.einsum("phfg,gphd->fphd", probs_b, v_heads, preferred_element_type=jnp.float32)
    delta = jnp.transpose(jnp.sum(g_heads.astype(jnp.float32) * attended, axis=-1), (1, 2, 0))
    grad_probs = jnp.einsum("fphd,gphd->phfg", g_heads, v_heads, preferred_element_type=jnp.float32)
    grad_scores = (probs * (grad_probs - delta[..., None])).astype(jnp.bfloat16)
    grad_value = jnp.einsum("phfg,fphd->gphd", probs_b, g_heads, preferred_element_type=jnp.float32)
    grad_query = (
        jnp.einsum("phfg,gphd->fphd", grad_scores, k_heads, preferred_element_type=jnp.float32)
        * scale
    )
    grad_key = (
        jnp.einsum("phfg,fphd->gphd", grad_scores, q_heads, preferred_element_type=jnp.float32)
        * scale
    )
    return (
        grad_query.astype(jnp.bfloat16),
        grad_key.astype(jnp.bfloat16),
        grad_value.astype(jnp.bfloat16),
    )


def per_device(query, key_in, value, grad_out, weights):
    tok_rows, width = query.shape
    head_count = width // HD

    def split_heads(array):
        return array.reshape(1, tok_rows, head_count, HD)

    sq = split_heads(query)
    sk = split_heads(key_in)
    sv = split_heads(value)
    sg = split_heads(grad_out)
    moved = (
        lax.all_to_all(sq, "tm", split_axis=1, concat_axis=0, tiled=True),
        lax.all_to_all(sk, "tm", split_axis=1, concat_axis=0, tiled=True),
        lax.all_to_all(sv, "tm", split_axis=1, concat_axis=0, tiled=True),
        lax.all_to_all(sg, "tm", split_axis=1, concat_axis=0, tiled=True),
    )
    grads = temporal(moved[0], moved[1], moved[2], moved[3])
    back = (
        lax.all_to_all(grads[0], "tm", split_axis=0, concat_axis=1, tiled=True),
        lax.all_to_all(grads[1], "tm", split_axis=0, concat_axis=1, tiled=True),
        lax.all_to_all(grads[2], "tm", split_axis=0, concat_axis=1, tiled=True),
    )
    stacked = jnp.stack(
        [
            back[0].reshape(tok_rows, width),
            back[1].reshape(tok_rows, width),
            back[2].reshape(tok_rows, width),
        ]
    )
    partial_sum = jnp.einsum(
        "mic,mtc->it",
        lax.all_gather(weights, "tm", axis=1, tiled=True),
        stacked,
        preferred_element_type=jnp.float32,
    )
    mine = lax.psum_scatter(partial_sum, "head", scatter_dimension=0, tiled=True)
    return mine.astype(jnp.bfloat16)


def solution(mesh):
    placed = (
        P("tm", "head"),
        P("tm", "head"),
        P("tm", "head"),
        P("tm", "head"),
        P(None, "tm", "head"),
    )
    return jax.shard_map(
        per_device, mesh=mesh, in_specs=placed, out_specs=P("head", "tm"), check_vma=False
    )
```

profile of v0, /device:TPU:1, one launch (start us, length us, event | category | flops | bytes accessed | tf_op | source)
XLA Modules:
  0.0 372.9 jit_solution(12953759409687776059)
XLA Ops:
  6.5 0.0 copy-start
  6.5 0.0 copy-start.1
  6.5 0.0 all-gather.2.cloned.1.call-start
  6.5 0.7 all-gather.2.cloned.1.call-update
  7.3 2.0 copy.45
  9.2 15.1 %all-to-all-start = ((bf16[1,256,8,128]{3,2,0,1:T(8,128)(2,1)}), bf16[1,256,8,128]{3,2,0,1:T(8,128)(2,1)S(1)}, u32[]{:S(2)}, u32[]{:S(2)}) async-start(bf16[1,256,8,128]{3,2,0,1:T(8,128)(2,1)} %bitcast.15), calls=%async_computation | async-start | bytes 1048576 | tf_op jit(solution)/shard_map/all_to_all | solution.py:48
  24.3 1.9 copy.46
  26.3 17.0 %all-to-all-done = bf16[1,256,8,128]{3,2,0,1:T(8,128)(2,1)S(1)} async-done(((bf16[1,256,8,128]{3,2,0,1:T(8,128)(2,1)}), bf16[1,256,8,128]{3,2,0,1:T(8,128)(2,1)S(1)}, u32[]{:S(2)}, u32[]{:S(2)}) %all-to-all-start) | async-done | bytes 524320 | tf_op jit(solution)/shard_map/all_to_all | solution.py:48
  43.3 9.4 %all-to-all-start.1 = ((bf16[1,256,8,128]{3,2,0,1:T(8,128)(2,1)}), bf16[1,256,8,128]{3,2,0,1:T(8,128)(2,1)S(1)}, u32[]{:S(2)}, u32[]{:S(2)}) async-start(bf16[1,256,8,128]{3,2,0,1:T(8,128)(2,1)} %bitcast.19), calls=%async_computation.1 | async-start | bytes 1048576 | tf_op jit(solution)/shard_map/all_to_all | solution.py:49
  52.6 0.0 copy-done
  52.7 0.9 copy.48
  53.6 13.5 %all-to-all-done.1 = bf16[1,256,8,128]{3,2,0,1:T(8,128)(2,1)S(1)} async-done(((bf16[1,256,8,128]{3,2,0,1:T(8,128)(2,1)}), bf16[1,256,8,128]{3,2,0,1:T(8,128)(2,1)S(1)}, u32[]{:S(2)}, u32[]{:S(2)}) %all-to-all-start.1) | async-done | bytes 524320 | tf_op jit(solution)/shard_map/all_to_all | solution.py:49
  67.0 4.9 %all-to-all-start.3 = ((bf16[1,256,8,128]{3,2,0,1:T(8,128)(2,1)}), bf16[1,256,8,128]{3,2,0,1:T(8,128)(2,1)S(1)}, u32[]{:S(2)}, u32[]{:S(2)}) async-start(bf16[1,256,8,128]{3,2,0,1:T(8,128)(2,1)} %bitcast.27), calls=%async_computation.3 | async-start | bytes 1048576 | tf_op jit(solution)/shard_map/all_to_all | solution.py:50
  71.9 0.0 copy-done.1
  71.9 0.9 copy.47
  72.8 30.1 %all-to-all-done.3 = bf16[1,256,8,128]{3,2,0,1:T(8,128)(2,1)S(1)} async-done(((bf16[1,256,8,128]{3,2,0,1:T(8,128)(2,1)}), bf16[1,256,8,128]{3,2,0,1:T(8,128)(2,1)S(1)}, u32[]{:S(2)}, u32[]{:S(2)}) %all-to-all-start.3) | async-done | bytes 524320 | tf_op jit(solution)/shard_map/all_to_all | solution.py:50
  103.0 6.8 %all-to-all-start.2 = ((bf16[1,256,8,128]{3,2,0,1:T(8,128)(2,1)}), bf16[1,256,8,128]{3,2,0,1:T(8,128)(2,1)S(1)}, u32[]{:S(2)}, u32[]{:S(2)}) async-start(bf16[1,256,8,128]{3,2,0,1:T(8,128)(2,1)} %bitcast.23), calls=%async_computation.2 | async-start | bytes 1048576 | tf_op jit(solution)/shard_map/all_to_all | solution.py:51
  109.7 0.6 fusion.39
  110.4 0.0 copy-start.2
  110.4 13.6 %all-to-all-done.2 = bf16[1,256,8,128]{3,2,0,1:T(8,128)(2,1)S(1)} async-done(((bf16[1,256,8,128]{3,2,0,1:T(8,128)(2,1)}), bf16[1,256,8,128]{3,2,0,1:T(8,128)(2,1)S(1)}, u32[]{:S(2)}, u32[]{:S(2)}) %all-to-all-start.2) | async-done | bytes 524320 | tf_op jit(solution)/shard_map/all_to_all | solution.py:51
  124.0 0.6 fusion.13
  124.6 0.0 copy-done.2
  124.6 2.1 fusion.10
  126.7 0.3 fusion.14
  127.0 1.1 copy.38
  128.2 5.9 %all-to-all-start.5 = ((bf16[64,4,8,128]{3,2,1,0:T(8,128)(2,1)}), bf16[64,4,8,128]{3,2,1,0:T(8,128)(2,1)S(1)}, u32[]{:S(2)}, u32[]{:S(2)}) async-start(bf16[64,4,8,128]{3,2,1,0:T(8,128)(2,1)} %copy.38), calls=%async_computation.5 | async-start | bytes 1048576 | tf_op jit(solution)/shard_map/all_to_all | solution.py:56
  134.1 0.4 fusion.15
  134.5 1.2 copy.36
  135.6 18.6 %all-to-all-done.5 = bf16[64,4,8,128]{3,2,1,0:T(8,128)(2,1)S(1)} async-done(((bf16[64,4,8,128]{3,2,1,0:T(8,128)(2,1)}), bf16[64,4,8,128]{3,2,1,0:T(8,128)(2,1)S(1)}, u32[]{:S(2)}, u32[]{:S(2)}) %all-to-all-start.5) | async-done | bytes 524320 | tf_op jit(solution)/shard_map/all_to_all | solution.py:56
  154.3 11.3 %all-to-all-start.4 = ((bf16[64,4,8,128]{3,2,1,0:T(8,128)(2,1)}), bf16[64,4,8,128]{3,2,1,0:T(8,128)(2,1)S(1)}, u32[]{:S(2)}, u32[]{:S(2)}) async-start(bf16[64,4,8,128]{3,2,1,0:T(8,128)(2,1)} %copy.36), calls=%async_computation.4 | async-start | bytes 1048576 | tf_op jit(solution)/shard_map/all_to_all | solution.py:55
  165.6 1.6 fusion.16
  167.2 1.1 copy.40
  168.3 17.4 %all-to-all-done.4 = bf16[64,4,8,128]{3,2,1,0:T(8,128)(2,1)S(1)} async-done(((bf16[64,4,8,128]{3,2,1,0:T(8,128)(2,1)}), bf16[64,4,8,128]{3,2,1,0:T(8,128)(2,1)S(1)}, u32[]{:S(2)}, u32[]{:S(2)}) %all-to-all-start.4) | async-done | bytes 524320 | tf_op jit(solution)/shard_map/all_to_all | solution.py:55
  185.7 6.5 %all-to-all-start.6 = ((bf16[64,4,8,128]{3,2,1,0:T(8,128)(2,1)}), bf16[64,4,8,128]{3,2,1,0:T(8,128)(2,1)S(1)}, u32[]{:S(2)}, u32[]{:S(2)}) async-start(bf16[64,4,8,128]{3,2,1,0:T(8,128)(2,1)} %copy.40), calls=%async_computation.6 | async-start | bytes 1048576 | tf_op jit(solution)/shard_map/all_to_all | solution.py:57
  192.3 0.2 reduce-scatter.2.cloned.1.call-start
  192.5 0.2 stack_reshape.10
  192.8 0.2 stack_reshape.9
  193.0 19.5 %all-to-all-done.6 = bf16[64,4,8,128]{3,2,1,0:T(8,128)(2,1)S(1)} async-done(((bf16[64,4,8,128]{3,2,1,0:T(8,128)(2,1)}), bf16[64,4,8,128]{3,2,1,0:T(8,128)(2,1)S(1)}, u32[]{:S(2)}, u32[]{:S(2)}) %all-to-all-start.6) | async-done | bytes 524320 | tf_op jit(solution)/shard_map/all_to_all | solution.py:57
  212.5 0.2 stack_reshape.11
  212.7 24.6 %all-gather.2.cloned.1.call-done = bf16[3,4096,1024]{2,1,0:T(8,128)(2,1)} async-done(((bf16[3,64,1024]{2,1,0:T(8,128)(2,1)}), bf16[3,4096,1024]{2,1,0:T(8,128)(2,1)}) %all-gather.2.cloned.1.call-update) | async-done | bytes 25165840 | tf_op jit(solution)/shard_map/all_gather | solution.py:68
  237.3 13.8 %convolution_bitcast_fusion = f32[4096,256]{0,1:T(8,128)} fusion(bf16[3,4096,1024]{2,1,0:T(8,128)(2,1)} %all-gather.2.cloned.1.call-done, bf16[1,256,1024]{2,1,0:T(8,128)(2,1)S(1)} %stack_reshape.11, bf16[1,256,1024]{2,1,0:T(8,128)(2,1)S(1)} %stack_reshape.10, bf16[1,256,1024]{2,1,0:T(8,128)(2,1)S(1)} %stack_reshape.9), kind=kOutput, calls=%fused_computation.1 | convolution fusion | flops 6444023808 | bytes 30932992 | tf_op jit(solution)/shard_map/mic,mtc->it/dot_general | solution.py:66
  251.1 0.0 reduce-scatter.2.cloned.1.call-update
  251.1 112.7 %reduce-scatter.2.cloned.1.call-done = f32[1024,256]{0,1:T(8,128)} async-done(((f32[4096,256]{0,1:T(8,128)}), f32[1024,256]{0,1:T(8,128)}) %reduce-scatter.2.cloned.1.call-update) | async-done | bytes 1048592 | tf_op jit(solution)/shard_map/reduce_scatter | solution.py:72
  363.8 1.3 convert_element_type.39
  365.1 1.0 copy.41
Async XLA Ops:
  6.5 46.1 %copy-start = (bf16[256,1024]{1,0:T(8,128)(2,1)S(1)}, bf16[256,1024]{1,0:T(8,128)(2,1)}, u32[]{:S(2)}) copy-start(bf16[256,1024]{1,0:T(8,128)(2,1)} %param.7) | copy-start | bytes 1572868
  6.5 65.4 %copy-start.1 = (bf16[256,1024]{1,0:T(8,128)(2,1)S(1)}, bf16[256,1024]{1,0:T(8,128)(2,1)}, u32[]{:S(2)}) copy-start(bf16[256,1024]{1,0:T(8,128)(2,1)} %param.8) | copy-start | bytes 1572868
  6.5 230.8 %all-gather.2.cloned.1.call-start = ((), (), s32[]{:S(2)}) async-start(), calls=%async_computation.8 | async-start | bytes 25559040 | tf_op jit(solution)/shard_map/all_gather | solution.py:68
  9.2 34.0 %all-to-all-start = ((bf16[1,256,8,128]{3,2,0,1:T(8,128)(2,1)}), bf16[1,256,8,128]{3,2,0,1:T(8,128)(2,1)S(1)}, u32[]{:S(2)}, u32[]{:S(2)}) async-start(bf16[1,256,8,128]{3,2,0,1:T(8,128)(2,1)} %bitcast.15), calls=%async_computation | async-start | bytes 1048576 | tf_op jit(solution)/shard_map/all_to_all | solution.py:48
  43.3 23.8 %all-to-all-start.1 = ((bf16[1,256,8,128]{3,2,0,1:T(8,128)(2,1)}), bf16[1,256,8,128]{3,2,0,1:T(8,128)(2,1)S(1)}, u32[]{:S(2)}, u32[]{:S(2)}) async-start(bf16[1,256,8,128]{3,2,0,1:T(8,128)(2,1)} %bitcast.19), calls=%async_computation.1 | async-start | bytes 1048576 | tf_op jit(solution)/shard_map/all_to_all | solution.py:49
  67.0 35.9 %all-to-all-start.3 = ((bf16[1,256,8,128]{3,2,0,1:T(8,128)(2,1)}), bf16[1,256,8,128]{3,2,0,1:T(8,128)(2,1)S(1)}, u32[]{:S(2)}, u32[]{:S(2)}) async-start(bf16[1,256,8,128]{3,2,0,1:T(8,128)(2,1)} %bitcast.27), calls=%async_computation.3 | async-start | bytes 1048576 | tf_op jit(solution)/shard_map/all_to_all | solution.py:50
  103.0 21.0 %all-to-all-start.2 = ((bf16[1,256,8,128]{3,2,0,1:T(8,128)(2,1)}), bf16[1,256,8,128]{3,2,0,1:T(8,128)(2,1)S(1)}, u32[]{:S(2)}, u32[]{:S(2)}) async-start(bf16[1,256,8,128]{3,2,0,1:T(8,128)(2,1)} %bitcast.23), calls=%async_computation.2 | async-start | bytes 1048576 | tf_op jit(solution)/shard_map/all_to_all | solution.py:51
  110.4 14.2 %copy-start.2 = (f32[4,8,64,64]{2,3,1,0:T(8,128)}, f32[4,8,64,64]{2,3,1,0:T(8,128)S(1)}, u32[]{:S(2)}) copy-start(f32[4,8,64,64]{2,3,1,0:T(8,128)S(1)} %get-tuple-element.6) | copy-start | bytes 1572868
  128.2 26.1 %all-to-all-start.5 = ((bf16[64,4,8,128]{3,2,1,0:T(8,128)(2,1)}), bf16[64,4,8,128]{3,2,1,0:T(8,128)(2,1)S(1)}, u32[]{:S(2)}, u32[]{:S(2)}) async-start(bf16[64,4,8,128]{3,2,1,0:T(8,128)(2,1)} %copy.38), calls=%async_computation.5 | async-start | bytes 1048576 | tf_op jit(solution)/shard_map/all_to_all | solution.py:56
  154.3 31.5 %all-to-all-start.4 = ((bf16[64,4,8,128]{3,2,1,0:T(8,128)(2,1)}), bf16[64,4,8,128]{3,2,1,0:T(8,128)(2,1)S(1)}, u32[]{:S(2)}, u32[]{:S(2)}) async-start(bf16[64,4,8,128]{3,2,1,0:T(8,128)(2,1)} %copy.36), calls=%async_computation.4 | async-start | bytes 1048576 | tf_op jit(solution)/shard_map/all_to_all | solution.py:55
  185.7 26.7 %all-to-all-start.6 = ((bf16[64,4,8,128]{3,2,1,0:T(8,128)(2,1)}), bf16[64,4,8,128]{3,2,1,0:T(8,128)(2,1)S(1)}, u32[]{:S(2)}, u32[]{:S(2)}) async-start(bf16[64,4,8,128]{3,2,1,0:T(8,128)(2,1)} %copy.40), calls=%async_computation.6 | async-start | bytes 1048576 | tf_op jit(solution)/shard_map/all_to_all | solution.py:57
  192.3 171.5 %reduce-scatter.2.cloned.1.call-start = ((), (), s32[]{:S(2)}) async-start(), calls=%async_computation.9 | async-start | bytes 5242880 | tf_op jit(solution)/shard_map/reduce_scatter | solution.py:72
Sparse Core Ops, SparseCore 0:
  10.7 226.5 all-gather.1
  251.2 112.5 reduce-scatter.1
where the time goes:
time: 374 us; the launch traced here: 373 us
  waiting for transfers between devices  268 us (72%)
  starting transfers between devices  60.2 us (16%)
  matrix products  19.4 us (5%)
  between operations  13.6 us (4%)
  local copies, waits for them, and re-layouts  10.8 us (3%)
    reduce_scatter x1, waiting for transfers between devices, per_device(): lax.psum_scatter(partial_sum, 'head', scatter_dimension=0, tiled=True)  113 us
    all_to_all x1, waiting for transfers between devices, per_device(): lax.all_to_all(sv, 'tm', split_axis=1, concat_axis=0, tiled=True)  30.1 us
    all_gather x1, waiting for transfers between devices, per_device(): lax.all_gather(weights, 'tm', axis=1, tiled=True)  24.6 us
    all_to_all x1, waiting for transfers between devices, per_device(): lax.all_to_all(grads[2], 'tm', split_axis=0, concat_axis=1, tiled=True)  19.5 us
    all_to_all x1, waiting for transfers between devices, per_device(): lax.all_to_all(grads[1], 'tm', split_axis=0, concat_axis=1, tiled=True)  18.6 us
    all_to_all x1, waiting for transfers between devices, per_device(): lax.all_to_all(grads[0], 'tm', split_axis=0, concat_axis=1, tiled=True)  17.4 us
    all_to_all x1, waiting for transfers between devices, per_device(): lax.all_to_all(sq, 'tm', split_axis=1, concat_axis=0, tiled=True)  17 us
    all_to_all x1, starting transfers between devices, per_device(): lax.all_to_all(sq, 'tm', split_axis=1, concat_axis=0, tiled=True)  15.1 us
  transfers between devices with their start and end apart: 9, of which 9 were waited for; matrix products, arithmetic and copies ran while one was open for 4% of the time, Pallas kernels for 0%

commit v1 on v0

--- a/solution.py
+++ b/solution.py
@@ -65,7 +65,9 @@
     )
     partial_sum = jnp.einsum(
         "mic,mtc->it",
-        lax.all_gather(weights, "tm", axis=1, tiled=True),
+        jnp.concatenate(
+            lax.all_to_all(jnp.stack([weights] * lax.axis_size("tm")), "tm", 0, 0), axis=1
+        ),
         stacked,
         preferred_element_type=jnp.float32,
     )

time: 374 us -> 828 us (2.21)
  waiting for transfers between devices: 268 us -> 681 us
  local copies, waits for them, and re-layouts: 10.8 us -> 39.7 us
  blocking collectives: 0 us -> 17.9 us
    all_to_all x1, waiting for transfers between devices: 17.4 us -> 531 us  [per_device(): lax.all_to_all(jnp.stack([weights] * lax.axis_size('tm')), 'tm', 0, 0)]
    reduce_scatter x1, waiting for transfers between devices: 113 us -> 69.2 us  [per_device(): lax.psum_scatter(partial_sum, 'head', scatter_dimension=0, tiled=True)]
    all_gather x1 -> x0, waiting for transfers between devices: 24.6 us -> none  [per_device(): lax.all_gather(weights, 'tm', axis=1, tiled=True)]
    reshape x0 -> x1, local copies, waits for them, and re-layouts: none -> 20.9 us  [per_device(): jnp.concatenate(lax.all_to_all(jnp.stack([weights] * lax.axis_size('tm'))...]
    all_to_all x1, waiting for transfers between devices: 30.1 us -> 10.4 us  [per_device(): lax.all_to_all(sv, 'tm', split_axis=1, concat_axis=0, tiled=True)]
    all_to_all x0 -> x1, blocking collectives: none -> 17.9 us  [per_device(): lax.all_to_all(grads[0], 'tm', split_axis=0, concat_axis=1, tiled=True)]
    all_to_all x1, waiting for transfers between devices: 19.5 us -> 9.82 us  [per_device(): lax.all_to_all(grads[2], 'tm', split_axis=0, concat_axis=1, tiled=True)]
    another operation x0 -> x1, local copies, waits for them, and re-layouts: none -> 8.73 us  [per_device(): jnp.stack([weights] * lax.axis_size('tm'))]
  transfers between devices with their start and end apart: 9 -> 8, of which waited for: 9 -> 8; matrix products, arithmetic and copies ran while one was open for 4% -> 2% of each run, Pallas kernels for 0% -> 0%
where the time goes in v1:
time: 828 us; the launch traced here: 827 us
  waiting for transfers between devices  681 us (82%)
  starting transfers between devices  53.8 us (6%)
  local copies, waits for them, and re-layouts  39.7 us (5%)
  matrix products  20.1 us (2%)
  blocking collectives  17.9 us (2%)
  between operations  13.6 us (2%)
    all_to_all x1, waiting for transfers between devices, per_device(): lax.all_to_all(jnp.stack([weights] * lax.axis_size('tm')), 'tm', 0, 0)  531 us
    reduce_scatter x1, waiting for transfers between devices, per_device(): lax.psum_scatter(partial_sum, 'head', scatter_dimension=0, tiled=True)  69.2 us
    reshape x1, local copies, waits for them, and re-layouts, per_device(): jnp.concatenate(lax.all_to_all(jnp.stack([weights] * lax.axis_size('tm'))...  20.9 us
    all_to_all x1, blocking collectives, per_device(): lax.all_to_all(grads[0], 'tm', split_axis=0, concat_axis=1, tiled=True)  17.9 us
    all_to_all x1, waiting for transfers between devices, per_device(): lax.all_to_all(sk, 'tm', split_axis=1, concat_axis=0, tiled=True)  17.4 us
  transfers between devices with their start and end apart: 8, of which 8 were waited for; matrix products, arithmetic and copies ran while one was open for 2% of the time, Pallas kernels for 0%

profile of v1, /device:TPU:1, one launch (start us, length us, event | category | flops | bytes accessed | tf_op | source)
XLA Modules:
  0.0 827.1 jit_solution(4864762090781597983)
XLA Ops:
  6.5 0.0 copy-start
  6.5 0.0 copy-start.1
  6.5 2.0 copy.48
  8.6 15.1 %all-to-all-start.2 = ((bf16[1,256,8,128]{3,2,0,1:T(8,128)(2,1)}), bf16[1,256,8,128]{3,2,0,1:T(8,128)(2,1)S(1)}, u32[]{:S(2)}, u32[]{:S(2)}) async-start(bf16[1,256,8,128]{3,2,0,1:T(8,128)(2,1)} %bitcast.25), calls=%async_computation.2 | async-start | bytes 1048576 | tf_op jit(solution)/shard_map/all_to_all | solution.py:51
  23.7 1.9 copy.47
  25.6 14.9 %all-to-all-done.2 = bf16[1,256,8,128]{3,2,0,1:T(8,128)(2,1)S(1)} async-done(((bf16[1,256,8,128]{3,2,0,1:T(8,128)(2,1)}), bf16[1,256,8,128]{3,2,0,1:T(8,128)(2,1)S(1)}, u32[]{:S(2)}, u32[]{:S(2)}) %all-to-all-start.2) | async-done | bytes 524320 | tf_op jit(solution)/shard_map/all_to_all | solution.py:51
  40.6 8.0 all-to-all-start.1
  48.5 0.0 copy-done
  48.5 0.9 copy.46
  49.4 17.4 %all-to-all-done.1 = bf16[1,256,8,128]{3,2,0,1:T(8,128)(2,1)S(1)} async-done(((bf16[1,256,8,128]{3,2,0,1:T(8,128)(2,1)}), bf16[1,256,8,128]{3,2,0,1:T(8,128)(2,1)S(1)}, u32[]{:S(2)}, u32[]{:S(2)}) %all-to-all-start.1) | async-done | bytes 524320 | tf_op jit(solution)/shard_map/all_to_all | solution.py:49
  66.8 6.5 all-to-all-start
  73.3 0.0 copy-done.1
  73.4 0.9 copy.49
  74.3 14.8 %all-to-all-done = bf16[1,256,8,128]{3,2,0,1:T(8,128)(2,1)S(1)} async-done(((bf16[1,256,8,128]{3,2,0,1:T(8,128)(2,1)}), bf16[1,256,8,128]{3,2,0,1:T(8,128)(2,1)S(1)}, u32[]{:S(2)}, u32[]{:S(2)}) %all-to-all-start) | async-done | bytes 524320 | tf_op jit(solution)/shard_map/all_to_all | solution.py:48
  89.1 6.9 all-to-all-start.3
  96.0 1.6 fusion.39
  97.6 1.6 fusion.16
  99.2 1.1 copy.40
  100.3 10.4 %all-to-all-done.3 = bf16[1,256,8,128]{3,2,0,1:T(8,128)(2,1)S(1)} async-done(((bf16[1,256,8,128]{3,2,0,1:T(8,128)(2,1)}), bf16[1,256,8,128]{3,2,0,1:T(8,128)(2,1)S(1)}, u32[]{:S(2)}, u32[]{:S(2)}) %all-to-all-start.3) | async-done | bytes 524320 | tf_op jit(solution)/shard_map/all_to_all | solution.py:50
  110.7 6.5 all-to-all-start.6
  117.3 0.0 copy-start.3
  117.3 1.9 fusion.13
  119.2 0.0 copy-done.3
  119.2 0.6 fusion.10
  119.8 0.0 copy-start.2
  119.8 0.3 fusion.14
  120.1 1.1 copy.38
  121.3 9.8 %all-to-all-done.6 = bf16[64,4,8,128]{3,2,1,0:T(8,128)(2,1)S(1)} async-done(((bf16[64,4,8,128]{3,2,1,0:T(8,128)(2,1)}), bf16[64,4,8,128]{3,2,1,0:T(8,128)(2,1)S(1)}, u32[]{:S(2)}, u32[]{:S(2)}) %all-to-all-start.6) | async-done | bytes 524320 | tf_op jit(solution)/shard_map/all_to_all | solution.py:57
  131.1 4.6 all-to-all-start.5
  135.7 0.4 fusion.15
  136.1 0.3 copy.36
  136.5 13.1 %all-to-all-done.5 = bf16[64,4,8,128]{3,2,1,0:T(8,128)(2,1)S(1)} async-done(((bf16[64,4,8,128]{3,2,1,0:T(8,128)(2,1)}), bf16[64,4,8,128]{3,2,1,0:T(8,128)(2,1)S(1)}, u32[]{:S(2)}, u32[]{:S(2)}) %all-to-all-start.5) | async-done | bytes 524320 | tf_op jit(solution)/shard_map/all_to_all | solution.py:56
  149.6 17.9 %all_to_all.80 = bf16[64,4,8,128]{3,2,1,0:T(8,128)(2,1)S(1)} all-to-all(bf16[64,4,8,128]{3,2,1,0:T(8,128)(2,1)S(1)} %copy.36), channel_id=1, replica_groups=mesh['tm'=64,'head'=4] {'tm'}, dimensions={0} | all-to-all | bytes 1048576 | tf_op jit(solution)/shard_map/all_to_all | solution.py:55
  167.4 0.0 copy-done.2
  167.4 8.7 %stack.5 = bf16[64,3,64,1024]{3,2,1,0:T(8,128)(2,1)} broadcast(bf16[3,64,1024]{2,1,0:T(8,128)(2,1)S(1)} %copy-done.2), dimensions={1,2,3} | broadcast | bytes 25559040 | tf_op jit(solution)/shard_map/stack | solution.py:69
  176.2 6.1 all-to-all-start.7
  182.3 0.0 reduce-scatter.2.cloned.1.call-start
  182.3 0.2 stack_reshape.11
  182.6 0.2 stack_reshape.10
  182.8 0.2 stack_reshape.9
  183.0 531.1 %all-to-all-done.7 = bf16[64,3,64,1024]{3,2,1,0:T(8,128)(2,1)} async-done(((bf16[64,3,64,1024]{3,2,1,0:T(8,128)(2,1)}), bf16[64,3,64,1024]{3,2,1,0:T(8,128)(2,1)}, u32[]{:S(2)}, u32[]{:S(2)}) %all-to-all-start.7) | async-done | bytes 25165856 | tf_op jit(solution)/shard_map/all_to_all | solution.py:69
  714.1 20.9 %copy.41 = bf16[3,64,64,1024]{3,2,1,0:T(8,128)(2,1)} copy(bf16[3,64,64,1024]{3,2,0,1:T(8,128)(2,1)} %bitcast.9) | data formatting | bytes 50331648 | tf_op jit(solution)/shard_map/reshape | solution.py:68
  735.0 13.8 %convolution_bitcast_fusion = f32[4096,256]{0,1:T(8,128)} fusion(bf16[3,4096,1024]{2,1,0:T(8,128)(2,1)} %bitcast.48, bf16[1,256,1024]{2,1,0:T(8,128)(2,1)S(1)} %stack_reshape.11, bf16[1,256,1024]{2,1,0:T(8,128)(2,1)S(1)} %stack_reshape.10, bf16[1,256,1024]{2,1,0:T(8,128)(2,1)S(1)} %stack_reshape.9), kind=kOutput, calls=%fused_computation.1 | convolution fusion | flops 6444023808 | bytes 30932992 | tf_op jit(solution)/shard_map/mic,mtc->it/dot_general | solution.py:66
  748.8 0.0 reduce-scatter.2.cloned.1.call-update
  748.8 69.2 %reduce-scatter.2.cloned.1.call-done = f32[1024,256]{0,1:T(8,128)} async-done(((f32[4096,256]{0,1:T(8,128)}), f32[1024,256]{0,1:T(8,128)}) %reduce-scatter.2.cloned.1.call-update) | async-done | bytes 1048592 | tf_op jit(solution)/shard_map/reduce_scatter | solution.py:74
  818.0 1.3 convert_element_type.39
  819.3 1.0 copy.42
Async XLA Ops:
  6.5 42.0 %copy-start = (bf16[256,1024]{1,0:T(8,128)(2,1)S(1)}, bf16[256,1024]{1,0:T(8,128)(2,1)}, u32[]{:S(2)}) copy-start(bf16[256,1024]{1,0:T(8,128)(2,1)} %param.5) | copy-start | bytes 1572868
  6.5 66.8 %copy-start.1 = (bf16[256,1024]{1,0:T(8,128)(2,1)S(1)}, bf16[256,1024]{1,0:T(8,128)(2,1)}, u32[]{:S(2)}) copy-start(bf16[256,1024]{1,0:T(8,128)(2,1)} %param.7) | copy-start | bytes 1572868
  8.6 32.0 %all-to-all-start.2 = ((bf16[1,256,8,128]{3,2,0,1:T(8,128)(2,1)}), bf16[1,256,8,128]{3,2,0,1:T(8,128)(2,1)S(1)}, u32[]{:S(2)}, u32[]{:S(2)}) async-start(bf16[1,256,8,128]{3,2,0,1:T(8,128)(2,1)} %bitcast.25), calls=%async_computation.2 | async-start | bytes 1048576 | tf_op jit(solution)/shard_map/all_to_all | solution.py:51
  40.6 26.3 %all-to-all-start.1 = ((bf16[1,256,8,128]{3,2,0,1:T(8,128)(2,1)}), bf16[1,256,8,128]{3,2,0,1:T(8,128)(2,1)S(1)}, u32[]{:S(2)}, u32[]{:S(2)}) async-start(bf16[1,256,8,128]{3,2,0,1:T(8,128)(2,1)} %bitcast.21), calls=%async_computation.1 | async-start | bytes 1048576 | tf_op jit(solution)/shard_map/all_to_all | solution.py:49
  66.8 22.3 %all-to-all-start = ((bf16[1,256,8,128]{3,2,0,1:T(8,128)(2,1)}), bf16[1,256,8,128]{3,2,0,1:T(8,128)(2,1)S(1)}, u32[]{:S(2)}, u32[]{:S(2)}) async-start(bf16[1,256,8,128]{3,2,0,1:T(8,128)(2,1)} %bitcast.17), calls=%async_computation | async-start | bytes 1048576 | tf_op jit(solution)/shard_map/all_to_all | solution.py:48
  89.1 21.6 %all-to-all-start.3 = ((bf16[1,256,8,128]{3,2,0,1:T(8,128)(2,1)}), bf16[1,256,8,128]{3,2,0,1:T(8,128)(2,1)S(1)}, u32[]{:S(2)}, u32[]{:S(2)}) async-start(bf16[1,256,8,128]{3,2,0,1:T(8,128)(2,1)} %bitcast.29), calls=%async_computation.3 | async-start | bytes 1048576 | tf_op jit(solution)/shard_map/all_to_all | solution.py:50
  110.7 20.4 %all-to-all-start.6 = ((bf16[64,4,8,128]{3,2,1,0:T(8,128)(2,1)}), bf16[64,4,8,128]{3,2,1,0:T(8,128)(2,1)S(1)}, u32[]{:S(2)}, u32[]{:S(2)}) async-start(bf16[64,4,8,128]{3,2,1,0:T(8,128)(2,1)} %copy.40), calls=%async_computation.6 | async-start | bytes 1048576 | tf_op jit(solution)/shard_map/all_to_all | solution.py:57
  117.3 2.0 copy-start.3
  119.8 47.6 %copy-start.2 = (bf16[3,64,1024]{2,1,0:T(8,128)(2,1)S(1)}, bf16[3,64,1024]{2,1,0:T(8,128)(2,1)}, u32[]{:S(2)}) copy-start(bf16[3,64,1024]{2,1,0:T(8,128)(2,1)} %param.9) | copy-start | bytes 1179652
  131.1 18.5 %all-to-all-start.5 = ((bf16[64,4,8,128]{3,2,1,0:T(8,128)(2,1)}), bf16[64,4,8,128]{3,2,1,0:T(8,128)(2,1)S(1)}, u32[]{:S(2)}, u32[]{:S(2)}) async-start(bf16[64,4,8,128]{3,2,1,0:T(8,128)(2,1)} %copy.38), calls=%async_computation.5 | async-start | bytes 1048576 | tf_op jit(solution)/shard_map/all_to_all | solution.py:56
  176.2 538.0 %all-to-all-start.7 = ((bf16[64,3,64,1024]{3,2,1,0:T(8,128)(2,1)}), bf16[64,3,64,1024]{3,2,1,0:T(8,128)(2,1)}, u32[]{:S(2)}, u32[]{:S(2)}) async-start(bf16[64,3,64,1024]{3,2,1,0:T(8,128)(2,1)} %stack.5), calls=%async_computation.7 | async-start | bytes 50331648 | tf_op jit(solution)/shard_map/all_to_all | solution.py:69
  182.3 635.7 %reduce-scatter.2.cloned.1.call-start = ((), (), s32[]{:S(2)}) async-start(), calls=%async_computation.9 | async-start | bytes 5242880 | tf_op jit(solution)/shard_map/reduce_scatter | solution.py:74
Sparse Core Ops, SparseCore 0:
  749.0 68.9 reduce-scatter.1
